TPU v7x, 256 devices: a whole 4x4x8 slice. The times are simulated.
256 devices in a mesh: row: 8 (over x, core), col: 32 (over z, y).
Axes of the slice: x: 4, y: 4, z: 8, core: 2. Of those that a mesh axis runs over, the one named last changes fastest.
Arguments:
- density: bfloat16 [256, 16, 128, 128], P(('row', 'col')), as said below
- cols: int32 [256, 16], replicated, may hold values from 0 to 255, as said below
Outputs:
- new_density: float32 [256, 16, 128, 128], P(('row', 'col'))
Inputs may be any that keep to these rules, and one draw needn't show every extreme that they name: Block row b is held by the device with row index (b) // 32 and col index q = (b) % 32. cols[b, 0] = b and a row's entries are distinct. For 1 <= t <= 7, cols[b, 2t - 1] is held by a device of col index q + t and cols[b, 2t] by one of col index q - t (modulo 32); cols[b, 15] by one of col index q + 16. The pattern is symmetric with mirrored slots: if j = cols[b, s] then cols[j, s'] = b, where s' = s for s = 0 and s = 15, s' = s + 1 for odd s below 15, and s' = s - 1 for even s above 0. density[b, s] is exactly the transpose of density[cols[b, s], s'], with s' the mirrored slot.
All inputs are finite; a program needn't handle non-finite values.
Results may differ from a plain program's by a relative error of at most 0.0093.
Values may be sent and summed in bfloat16 or wider, within the bound.
No kernel may reach another device: no remote copies, remote signals or barrier semaphores. Data moves between devices by JAX's collectives and lax.ppermute only.
A program may use at most 128 MiB of HBM per device.

v0:
```python
import jax
import jax.numpy as jnp
from jax import lax
from jax.sharding import PartitionSpec as P


def shifted(value, axis, by):
    length = lax.axis_size(axis)
    return lax.ppermute(value, axis, [(i, (i + by) % length) for i in range(length)])


def slot_offsets(slot_count, grid_cols):
    offsets = [0]
    for stride in range(1, (slot_count - 2) // 2 + 1):
        offsets = offsets + [stride, -stride]
    return offsets + [grid_cols // 2]


def mirror_slots(slot_count):
    order = [0]
    for stride in range(1, (slot_count - 2) // 2 + 1):
        order = order + [2 * stride, 2 * stride - 1]
    return order + [slot_count - 1]


def per_device(density, cols):
    rows_here = density.shape[0]
    slot_count = density.shape[1]
    grid_cols = lax.axis_size("col")
    my_row = lax.axis_index("row")
    my_col = lax.axis_index("col")
    offsets = slot_offsets(slot_count, grid_cols)
    mirror = jnp.array(mirror_slots(slot_count), jnp.int32)
    shift_ids = jnp.array(offsets, jnp.int32)
    local_ids = jnp.arange(rows_here, dtype=jnp.int32)
    slot_ids = jnp.arange(slot_count, dtype=jnp.int32)
    source_col = (my_col - shift_ids) % grid_cols
    tile_rows = (my_row * grid_cols + source_col)[:, None] * rows_here + local_ids[None, :]
    left_cols = cols[tile_rows]
    targets = left_cols[slot_ids[:, None], local_ids[None, :], slot_ids[:, None]]
    target_cols = cols[targets]
    matches = left_cols[..., :, None] == target_cols[..., None, :]
    present = jnp.any(matches, axis=-1)
    found_slot = jnp.sum(jnp.where(matches, slot_ids, 0), axis=-1)
    target_rank = targets // rows_here // grid_cols * rows_here + targets % rows_here
    present_mask = present[..., None, None]
    gathered = lax.all_gather(density, "col", axis=0, tiled=True)
    left_blocks = gathered[source_col[:, None] * rows_here + local_ids[None, :]]
    column_blocks = lax.all_gather(density, "row", axis=0, tiled=True)
    right_blocks = column_blocks[target_rank[:, :, None], found_slot]
    right_blocks = jnp.where(present_mask, right_blocks, jnp.zeros((), right_blocks.dtype))
    square_tile = jnp.einsum(
        "sltab,sltcb->slac", left_blocks, right_blocks, preferred_element_type=jnp.float32
    )
    square_half = square_tile.astype(jnp.bfloat16)
    square_panel = lax.all_gather(square_half[None], "row", axis=0, tiled=True)
    inner_row = left_cols // rows_here // grid_cols
    inner_local = left_cols % rows_here
    from_square = square_panel[inner_row, mirror[found_slot], inner_local]
    from_square = jnp.where(present_mask, from_square, jnp.zeros((), from_square.dtype))
    cube_tile = jnp.einsum(
        "sltab,sltbc->slac", left_blocks, from_square, preferred_element_type=jnp.float32
    )
    new_tiles = 3.0 * square_tile - 2.0 * cube_tile
    returned_pieces = []
    for position, stride in enumerate(offsets):
        if stride == 0:
            returned_pieces.append(new_tiles[position])
        else:
            returned_pieces.append(shifted(new_tiles[position], "col", -stride))
    return jnp.stack(returned_pieces, axis=1)


def solution(mesh):
    in_specs = (P(("row", "col"), None, None, None), P())
    out_specs = P(("row", "col"), None, None, None)
    return jax.shard_map(
        per_device, mesh=mesh, in_specs=in_specs, out_specs=out_specs, check_vma=False
    )
```

profile of v0, /device:TPU:48, one launch (start us, length us, event | category | flops | bytes accessed | tf_op | source)
XLA Modules:
  0.0 314.3 jit_solution(2974334684125972960)
XLA Ops:
  6.5 0.7 all-gather.7.cloned.1.call-update
  8.1 0.8 copy.11
  12.5 33.8 %all-gather.7.cloned.1.call-done = bf16[8,16,128,128]{3,2,1,0:T(8,128)(2,1)} async-done(((bf16[1,16,128,128]{3,2,1,0:T(8,128)(2,1)}), bf16[8,16,128,128]{3,2,1,0:T(8,128)(2,1)}) %all-gather.7.cloned.1.call-update) | async-done | bytes 4194320 | tf_op jit(solution)/shard_map/all_gather | solution.py:49
  46.3 12.1 %gather_fusion.4 = bf16[256,128,128]{2,1,0:T(8,128)(2,1)} fusion(bf16[8,16,128,128]{3,2,1,0:T(8,128)(2,1)} %all-gather.7.cloned.1.call-done, s32[256]{0:T(256)S(1)} %reshape.430), kind=kCustom, calls=%fused_computation.4 | custom fusion | bytes 16779264 | tf_op jit(solution)/shard_map/gather | solution.py:50
  58.4 127.8 %all-gather.5.cloned.1.call-done = bf16[32,16,128,128]{3,2,1,0:T(8,128)(2,1)} async-done(((bf16[1,16,128,128]{3,2,1,0:T(8,128)(2,1)}), bf16[32,16,128,128]{3,2,1,0:T(8,128)(2,1)}) %all-gather.5.cloned.1.call-update) | async-done | bytes 16777232 | tf_op jit(solution)/shard_map/all_gather | solution.py:47
  186.2 10.6 %gather_fusion = bf16[16,16,128,128]{3,2,1,0:T(8,128)(2,1)} fusion(bf16[32,16,128,128]{3,2,1,0:T(8,128)(2,1)} %all-gather.5.cloned.1.call-done, s32[1024]{0:T(1024)S(1)} %pad_clamp_fusion.3), kind=kCustom, calls=%fused_computation | custom fusion | bytes 16777280 | tf_op jit(solution)/shard_map/gather | solution.py:48
  196.8 9.0 %fusion.38 = (bf16[16,128,128]{2,1,0:T(8,128)(2,1)}, f32[16,128,128]{2,1,0:T(8,128)S(1)}) fusion(bf16[16,16,128,128]{3,2,1,0:T(8,128)(2,1)} %gather_fusion, bf16[16,16,128,128]{3,2,1,0:T(8,128)(2,1)} %bitcast.90, pred[16,16]{1,0:T(8,128)(4,1)S(1)} %compare_reduce_fusion), kind=kOutput, calls=%fused_computation.88 | convolution fusion | flops 1078198272 | bytes 18350336 | tf_op jit(solution)/shard_map/sltab,sltcb->slac/dot_general | solution.py:52
  205.9 1.9 gather_fusion.5
  208.0 33.0 %all-gather.9.cloned.1.call-done = bf16[128,128,128]{2,1,0:T(8,128)(2,1)} async-done(((bf16[16,128,128]{2,1,0:T(8,128)(2,1)}), bf16[128,128,128]{2,1,0:T(8,128)(2,1)}) %all-gather.9.cloned.1.call-update) | async-done | bytes 4194320 | tf_op jit(solution)/shard_map/all_gather | solution.py:56
  241.0 12.2 %gather_fusion.6 = bf16[256,128,128]{2,1,0:T(8,128)(2,1)} fusion(bf16[8,16,1,128,128]{4,3,1,0,2:T(8,128)(2,1)} %bitcast.89, s32[256]{0:T(256)S(1)} %reshape.446), kind=kCustom, calls=%fused_computation.6 | custom fusion | bytes 16780288 | tf_op jit(solution)/shard_map/gather | solution.py:59
  253.2 8.2 %fusion.17 = f32[16,128,128]{2,1,0:T(8,128)S(1)} fusion(bf16[16,16,128,128]{3,2,1,0:T(8,128)(2,1)} %gather_fusion, bf16[16,16,128,128]{3,2,1,0:T(8,128)(2,1)} %bitcast.91, pred[16,16]{1,0:T(8,128)(4,1)S(1)} %compare_reduce_fusion, f32[16,128,128]{2,1,0:T(8,128)S(1)} %get-tuple-element.23), kind=kOutput, calls=%fused_computation.18 | convolution fusion | flops 1078722560 | bytes 18874624 | tf_op jit(solution)/shard_map/sltab,sltbc->slac/dot_general | solution.py:61
  261.5 0.8 collective-permute-start
  262.3 1.5 collective-permute-start.1
  263.8 1.2 collective-permute-start.2
  265.0 3.2 %collective-permute-start.3 = (f32[1,128,128]{2,1,0:T(8,128)S(1)}, f32[1,128,128]{2,1,0:T(8,128)S(1)}, u32[]{:S(2)}, u32[]{:S(2)}) collective-permute-start(f32[1,128,128]{2,1,0:T(8,128)S(1)} %get-tuple-element.18), channel_id=1, source_target_pairs={{0,2},{1,3},{2,4},{3,5},{4,6},{5,7},{6,8},{7,9},{8,10},{9,11},{10,... | collective-permute-start | bytes 196616 | tf_op jit(solution)/shard_map/ppermute | solution.py:9
  268.3 3.2 %collective-permute-start.4 = (f32[1,128,128]{2,1,0:T(8,128)S(1)}, f32[1,128,128]{2,1,0:T(8,128)S(1)}, u32[]{:S(2)}, u32[]{:S(2)}) collective-permute-start(f32[1,128,128]{2,1,0:T(8,128)S(1)} %get-tuple-element.17), channel_id=1, source_target_pairs={{0,29},{1,30},{2,31},{3,0},{4,1},{5,2},{6,3},{7,4},{8,5},{9,6},{10... | collective-permute-start | bytes 196616 | tf_op jit(solution)/shard_map/ppermute | solution.py:9
  271.4 5.9 %collective-permute-start.6 = (f32[1,128,128]{2,1,0:T(8,128)S(1)}, f32[1,128,128]{2,1,0:T(8,128)S(1)}, u32[]{:S(2)}, u32[]{:S(2)}) collective-permute-start(f32[1,128,128]{2,1,0:T(8,128)S(1)} %get-tuple-element.15), channel_id=1, source_target_pairs={{0,28},{1,29},{2,30},{3,31},{4,0},{5,1},{6,2},{7,3},{8,4},{9,5},{1... | collective-permute-start | bytes 196616 | tf_op jit(solution)/shard_map/ppermute | solution.py:9
  277.4 3.4 %collective-permute-start.8 = (f32[1,128,128]{2,1,0:T(8,128)S(1)}, f32[1,128,128]{2,1,0:T(8,128)S(1)}, u32[]{:S(2)}, u32[]{:S(2)}) collective-permute-start(f32[1,128,128]{2,1,0:T(8,128)S(1)} %get-tuple-element.13), channel_id=1, source_target_pairs={{0,27},{1,28},{2,29},{3,30},{4,31},{5,0},{6,1},{7,2},{8,3},{9,4},{... | collective-permute-start | bytes 196616 | tf_op jit(solution)/shard_map/ppermute | solution.py:9
  281.1 3.7 %collective-permute-start.10 = (f32[1,128,128]{2,1,0:T(8,128)S(1)}, f32[1,128,128]{2,1,0:T(8,128)S(1)}, u32[]{:S(2)}, u32[]{:S(2)}) collective-permute-start(f32[1,128,128]{2,1,0:T(8,128)S(1)} %get-tuple-element.11), channel_id=1, source_target_pairs={{0,26},{1,27},{2,28},{3,29},{4,30},{5,31},{6,0},{7,1},{8,2},{9,3},... | collective-permute-start | bytes 196616 | tf_op jit(solution)/shard_map/ppermute | solution.py:9
  284.8 1.7 collective-permute-start.11
  286.6 10.8 %collective-permute-start.12 = (f32[1,128,128]{2,1,0:T(8,128)S(1)}, f32[1,128,128]{2,1,0:T(8,128)S(1)}, u32[]{:S(2)}, u32[]{:S(2)}) collective-permute-start(f32[1,128,128]{2,1,0:T(8,128)S(1)} %get-tuple-element.9), channel_id=1, source_target_pairs={{0,25},{1,26},{2,27},{3,28},{4,29},{5,30},{6,31},{7,0},{8,1},{9,2}... | collective-permute-start | bytes 196616 | tf_op jit(solution)/shard_map/ppermute | solution.py:9
  297.6 3.0 collective-permute-start.14
  300.6 5.5 %collective-permute-done.13 = f32[1,128,128]{2,1,0:T(8,128)S(1)} collective-permute-done((f32[1,128,128]{2,1,0:T(8,128)S(1)}, f32[1,128,128]{2,1,0:T(8,128)S(1)}, u32[]{:S(2)}, u32[]{:S(2)}) %collective-permute-start.13) | collective-permute-done | bytes 65568 | tf_op jit(solution)/shard_map/ppermute | solution.py:9
  306.1 1.0 copy-done.1
  (72 shorter events, 5.8 us)
Async XLA Ops:
  6.5 39.8 %all-gather.7.cloned.1.call-start = ((), (), s32[]{:S(2)}) async-start(), calls=%async_computation.1 | async-start | bytes 4718592 | tf_op jit(solution)/shard_map/all_gather | solution.py:49
  7.3 179.0 %all-gather.5.cloned.1.call-start = ((), (), s32[]{:S(2)}) async-start(), calls=%async_computation | async-start | bytes 17301504 | tf_op jit(solution)/shard_map/all_gather | solution.py:47
  8.0 233.0 %all-gather.9.cloned.1.call-start = ((), (), s32[]{:S(2)}) async-start(), calls=%async_computation.2 | async-start | bytes 4718592 | tf_op jit(solution)/shard_map/all_gather | solution.py:56
  196.8 9.1 %copy-start = (s32[16]{0:T(128)S(1)}, s32[16]{0:T(128)}, u32[]{:S(2)}) copy-start(s32[16]{0:T(128)} %constant.115.clone) | copy-start | bytes 196
  261.5 9.9 %collective-permute-start = (f32[1,128,128]{2,1,0:T(8,128)S(1)}, f32[1,128,128]{2,1,0:T(8,128)S(1)}, u32[]{:S(2)}, u32[]{:S(2)}) collective-permute-start(f32[1,128,128]{2,1,0:T(8,128)S(1)} %get-tuple-element.21), channel_id=1, source_target_pairs={{0,31},{1,0},{2,1},{3,2},{4,3},{5,4},{6,5},{7,6},{8,7},{9,8},{10,9... | collective-permute-start | bytes 196616 | tf_op jit(solution)/shard_map/ppermute | solution.py:9
  262.3 9.1 %collective-permute-start.1 = (f32[1,128,128]{2,1,0:T(8,128)S(1)}, f32[1,128,128]{2,1,0:T(8,128)S(1)}, u32[]{:S(2)}, u32[]{:S(2)}) collective-permute-start(f32[1,128,128]{2,1,0:T(8,128)S(1)} %get-tuple-element.20), channel_id=1, source_target_pairs={{0,1},{1,2},{2,3},{3,4},{4,5},{5,6},{6,7},{7,8},{8,9},{9,10},{10,1... | collective-permute-start | bytes 196616 | tf_op jit(solution)/shard_map/ppermute | solution.py:9
  263.8 13.5 %collective-permute-start.2 = (f32[1,128,128]{2,1,0:T(8,128)S(1)}, f32[1,128,128]{2,1,0:T(8,128)S(1)}, u32[]{:S(2)}, u32[]{:S(2)}) collective-permute-start(f32[1,128,128]{2,1,0:T(8,128)S(1)} %get-tuple-element.19), channel_id=1, source_target_pairs={{0,30},{1,31},{2,0},{3,1},{4,2},{5,3},{6,4},{7,5},{8,6},{9,7},{10,... | collective-permute-start | bytes 196616 | tf_op jit(solution)/shard_map/ppermute | solution.py:9
  265.0 12.4 %collective-permute-start.3 = (f32[1,128,128]{2,1,0:T(8,128)S(1)}, f32[1,128,128]{2,1,0:T(8,128)S(1)}, u32[]{:S(2)}, u32[]{:S(2)}) collective-permute-start(f32[1,128,128]{2,1,0:T(8,128)S(1)} %get-tuple-element.18), channel_id=1, source_target_pairs={{0,2},{1,3},{2,4},{3,5},{4,6},{5,7},{6,8},{7,9},{8,10},{9,11},{10,... | collective-permute-start | bytes 196616 | tf_op jit(solution)/shard_map/ppermute | solution.py:9
  268.3 12.6 %collective-permute-start.4 = (f32[1,128,128]{2,1,0:T(8,128)S(1)}, f32[1,128,128]{2,1,0:T(8,128)S(1)}, u32[]{:S(2)}, u32[]{:S(2)}) collective-permute-start(f32[1,128,128]{2,1,0:T(8,128)S(1)} %get-tuple-element.17), channel_id=1, source_target_pairs={{0,29},{1,30},{2,31},{3,0},{4,1},{5,2},{6,3},{7,4},{8,5},{9,6},{10... | collective-permute-start | bytes 196616 | tf_op jit(solution)/shard_map/ppermute | solution.py:9
  271.4 9.6 %collective-permute-start.5 = (f32[1,128,128]{2,1,0:T(8,128)S(1)}, f32[1,128,128]{2,1,0:T(8,128)S(1)}, u32[]{:S(2)}, u32[]{:S(2)}) collective-permute-start(f32[1,128,128]{2,1,0:T(8,128)S(1)} %get-tuple-element.16), channel_id=1, source_target_pairs={{0,3},{1,4},{2,5},{3,6},{4,7},{5,8},{6,9},{7,10},{8,11},{9,12},{10... | collective-permute-start | bytes 196616 | tf_op jit(solution)/shard_map/ppermute | solution.py:9
  271.4 13.4 %collective-permute-start.6 = (f32[1,128,128]{2,1,0:T(8,128)S(1)}, f32[1,128,128]{2,1,0:T(8,128)S(1)}, u32[]{:S(2)}, u32[]{:S(2)}) collective-permute-start(f32[1,128,128]{2,1,0:T(8,128)S(1)} %get-tuple-element.15), channel_id=1, source_target_pairs={{0,28},{1,29},{2,30},{3,31},{4,0},{5,1},{6,2},{7,3},{8,4},{9,5},{1... | collective-permute-start | bytes 196616 | tf_op jit(solution)/shard_map/ppermute | solution.py:9
  277.3 9.3 %collective-permute-start.7 = (f32[1,128,128]{2,1,0:T(8,128)S(1)}, f32[1,128,128]{2,1,0:T(8,128)S(1)}, u32[]{:S(2)}, u32[]{:S(2)}) collective-permute-start(f32[1,128,128]{2,1,0:T(8,128)S(1)} %get-tuple-element.14), channel_id=1, source_target_pairs={{0,4},{1,5},{2,6},{3,7},{4,8},{5,9},{6,10},{7,11},{8,12},{9,13},{1... | collective-permute-start | bytes 196616 | tf_op jit(solution)/shard_map/ppermute | solution.py:9
  277.4 20.0 %collective-permute-start.8 = (f32[1,128,128]{2,1,0:T(8,128)S(1)}, f32[1,128,128]{2,1,0:T(8,128)S(1)}, u32[]{:S(2)}, u32[]{:S(2)}) collective-permute-start(f32[1,128,128]{2,1,0:T(8,128)S(1)} %get-tuple-element.13), channel_id=1, source_target_pairs={{0,27},{1,28},{2,29},{3,30},{4,31},{5,0},{6,1},{7,2},{8,3},{9,4},{... | collective-permute-start | bytes 196616 | tf_op jit(solution)/shard_map/ppermute | solution.py:9
  280.9 16.7 %collective-permute-start.9 = (f32[1,128,128]{2,1,0:T(8,128)S(1)}, f32[1,128,128]{2,1,0:T(8,128)S(1)}, u32[]{:S(2)}, u32[]{:S(2)}) collective-permute-start(f32[1,128,128]{2,1,0:T(8,128)S(1)} %get-tuple-element.12), channel_id=1, source_target_pairs={{0,5},{1,6},{2,7},{3,8},{4,9},{5,10},{6,11},{7,12},{8,13},{9,14},{... | collective-permute-start | bytes 196616 | tf_op jit(solution)/shard_map/ppermute | solution.py:9
  281.1 19.5 %collective-permute-start.10 = (f32[1,128,128]{2,1,0:T(8,128)S(1)}, f32[1,128,128]{2,1,0:T(8,128)S(1)}, u32[]{:S(2)}, u32[]{:S(2)}) collective-permute-start(f32[1,128,128]{2,1,0:T(8,128)S(1)} %get-tuple-element.11), channel_id=1, source_target_pairs={{0,26},{1,27},{2,28},{3,29},{4,30},{5,31},{6,0},{7,1},{8,2},{9,3},... | collective-permute-start | bytes 196616 | tf_op jit(solution)/shard_map/ppermute | solution.py:9
  284.8 15.7 %collective-permute-start.11 = (f32[1,128,128]{2,1,0:T(8,128)S(1)}, f32[1,128,128]{2,1,0:T(8,128)S(1)}, u32[]{:S(2)}, u32[]{:S(2)}) collective-permute-start(f32[1,128,128]{2,1,0:T(8,128)S(1)} %get-tuple-element.10), channel_id=1, source_target_pairs={{0,6},{1,7},{2,8},{3,9},{4,10},{5,11},{6,12},{7,13},{8,14},{9,15},... | collective-permute-start | bytes 196616 | tf_op jit(solution)/shard_map/ppermute | solution.py:9
  286.6 14.0 %collective-permute-start.12 = (f32[1,128,128]{2,1,0:T(8,128)S(1)}, f32[1,128,128]{2,1,0:T(8,128)S(1)}, u32[]{:S(2)}, u32[]{:S(2)}) collective-permute-start(f32[1,128,128]{2,1,0:T(8,128)S(1)} %get-tuple-element.9), channel_id=1, source_target_pairs={{0,25},{1,26},{2,27},{3,28},{4,29},{5,30},{6,31},{7,0},{8,1},{9,2}... | collective-permute-start | bytes 196616 | tf_op jit(solution)/shard_map/ppermute | solution.py:9
  297.4 8.7 %collective-permute-start.13 = (f32[1,128,128]{2,1,0:T(8,128)S(1)}, f32[1,128,128]{2,1,0:T(8,128)S(1)}, u32[]{:S(2)}, u32[]{:S(2)}) collective-permute-start(f32[1,128,128]{2,1,0:T(8,128)S(1)} %get-tuple-element.8), channel_id=1, source_target_pairs={{0,7},{1,8},{2,9},{3,10},{4,11},{5,12},{6,13},{7,14},{8,15},{9,16}... | collective-permute-start | bytes 196616 | tf_op jit(solution)/shard_map/ppermute | solution.py:9
  297.6 8.6 %collective-permute-start.14 = (f32[1,128,128]{2,1,0:T(8,128)S(1)}, f32[1,128,128]{2,1,0:T(8,128)S(1)}, u32[]{:S(2)}, u32[]{:S(2)}) collective-permute-start(f32[1,128,128]{2,1,0:T(8,128)S(1)} %get-tuple-element.7), channel_id=1, source_target_pairs={{0,16},{1,17},{2,18},{3,19},{4,20},{5,21},{6,22},{7,23},{8,24},{9,... | collective-permute-start | bytes 196616 | tf_op jit(solution)/shard_map/ppermute | solution.py:9
  306.1 1.0 copy-start.1
Sparse Core Ops, SparseCore 0:
  9.2 37.0 all-gather.6
  48.9 137.2 all-gather.4
  205.9 35.0 all-gather.8
where the time goes:
time: 314 us
  waiting for transfers between devices  202 us (64%)
  local copies, waits for them, and re-layouts  41.5 us (13%)
  starting transfers between devices  38.9 us (12%)
  matrix products  17.2 us (5%)
  between operations  13.4 us (4%)
    all_gather x1, waiting for transfers between devices, per_device(): gathered = lax.all_gather(density, 'col', axis=0, tiled=True)  128 us
    ppermute x15, starting transfers between devices, shifted(): lax.ppermute(value, axis, [(i, (i + by) % length) for i in range(length)])  38.8 us
    all_gather x1, waiting for transfers between devices, per_device(): column_blocks = lax.all_gather(density, 'row', axis=0, tiled=True)  33.8 us
    all_gather x1, waiting for transfers between devices, per_device(): square_panel = lax.all_gather(square_half[None], 'row', axis=0, tiled=True)  33 us
    gather x3, local copies, waits for them, and re-layouts, per_device(): from_square = square_panel[inner_row, mirror[found_slot], inner_local]  14.2 us
    gather x1, local copies, waits for them, and re-layouts, per_device(): right_blocks = column_blocks[target_rank[:, :, None], found_slot]  12.1 us
    gather x1, local copies, waits for them, and re-layouts, per_device(): left_blocks = gathered[source_col[:, None] * rows_here + local_ids[None, :]]  10.6 us
    dot_general x1, matrix products, per_device(): jnp.einsum('sltab,sltcb->slac', left_blocks, right_blocks, preferred_elem...  8.99 us
  transfers between devices with their start and end apart: 18, of which 4 were waited for; matrix products, arithmetic and copies ran while one was open for 6% of the time, Pallas kernels for 0%

commit v1 on v0

--- a/solution.py
+++ b/solution.py
@@ -46,7 +46,9 @@
     present_mask = present[..., None, None]
     gathered = lax.all_gather(density, "col", axis=0, tiled=True)
     left_blocks = gathered[source_col[:, None] * rows_here + local_ids[None, :]]
-    column_blocks = lax.all_gather(density, "row", axis=0, tiled=True)
+    column_blocks = jnp.concatenate(
+        lax.all_to_all(jnp.stack([density] * lax.axis_size("row")), "row", 0, 0), axis=0
+    )
     right_blocks = column_blocks[target_rank[:, :, None], found_slot]
     right_blocks = jnp.where(present_mask, right_blocks, jnp.zeros((), right_blocks.dtype))
     square_tile = jnp.einsum(

time: 314 us -> 278 us (0.89)
  waiting for transfers between devices: 202 us -> 157 us
  starting transfers between devices: 38.9 us -> 43.4 us
  local copies, waits for them, and re-layouts: 41.5 us -> 45.7 us
    all_gather x1, waiting for transfers between devices: 128 us -> 71.2 us  [per_device(): gathered = lax.all_gather(density, 'col', axis=0, tiled=True)]
    all_to_all x0 -> x1, waiting for transfers between devices: none -> 46.5 us  [per_device(): lax.all_to_all(jnp.stack([density] * lax.axis_size('row')), 'row', 0, 0)]
    all_gather x1 -> x0, waiting for transfers between devices: 33.8 us -> none  [per_device(): column_blocks = lax.all_gather(density, 'row', axis=0, tiled=True)]
    all_to_all x0 -> x1, starting transfers between devices: none -> 4.55 us  [per_device(): lax.all_to_all(jnp.stack([density] * lax.axis_size('row')), 'row', 0, 0)]
    another operation x0 -> x1, local copies, waits for them, and re-layouts: none -> 4.11 us  [per_device(): jnp.stack([density] * lax.axis_size('row'))]
  transfers between devices with their start and end apart: 18 -> 18, of which waited for: 4 -> 4; matrix products, arithmetic and copies ran while one was open for 6% -> 8% of each run, Pallas kernels for 0% -> 0%
where the time goes in v1:
time: 278 us
  waiting for transfers between devices  157 us (56%)
  local copies, waits for them, and re-layouts  45.7 us (16%)
  starting transfers between devices  43.4 us (16%)
  matrix products  17.2 us (6%)
  between operations  13.7 us (5%)
    all_gather x1, waiting for transfers between devices, per_device(): gathered = lax.all_gather(density, 'col', axis=0, tiled=True)  71.2 us
    all_to_all x1, waiting for transfers between devices, per_device(): lax.all_to_all(jnp.stack([density] * lax.axis_size('row')), 'row', 0, 0)  46.5 us
    ppermute x15, starting transfers between devices, shifted(): lax.ppermute(value, axis, [(i, (i + by) % length) for i in range(length)])  38.8 us
    all_gather x1, waiting for transfers between devices, per_device(): square_panel = lax.all_gather(square_half[None], 'row', axis=0, tiled=True)  33 us
    gather x3, local copies, waits for them, and re-layouts, per_device(): from_square = square_panel[inner_row, mirror[found_slot], inner_local]  14.2 us
    gather x1, local copies, waits for them, and re-layouts, per_device(): right_blocks = column_blocks[target_rank[:, :, None], found_slot]  12.9 us
    gather x1, local copies, waits for them, and re-layouts, per_device(): left_blocks = gathered[source_col[:, None] * rows_here + local_ids[None, :]]  10.6 us
    dot_general x1, matrix products, per_device(): jnp.einsum('sltab,sltcb->slac', left_blocks, right_blocks, preferred_elem...  8.99 us
  transfers between devices with their start and end apart: 18, of which 4 were waited for; matrix products, arithmetic and copies ran while one was open for 8% of the time, Pallas kernels for 0%

profile of v1, /device:TPU:48, one launch (start us, length us, event | category | flops | bytes accessed | tf_op | source)
XLA Modules:
  0.0 278.1 jit_solution(8824874548975398144)
XLA Ops:
  7.3 4.1 %stack.59 = bf16[8,1,16,128,128]{4,3,2,1,0:T(8,128)(2,1)} broadcast(bf16[16,128,128]{2,1,0:T(8,128)(2,1)} %bitcast.94), dimensions={2,3,4} | broadcast | bytes 4718592 | tf_op jit(solution)/shard_map/stack | solution.py:50
  11.4 4.6 %all-to-all-start = ((bf16[8,1,16,128,128]{4,3,2,1,0:T(8,128)(2,1)}), bf16[8,1,16,128,128]{4,3,2,1,0:T(8,128)(2,1)}, u32[]{:S(2)}, u32[]{:S(2)}) async-start(bf16[8,1,16,128,128]{4,3,2,1,0:T(8,128)(2,1)} %stack.59), calls=%async_computation | async-start | bytes 8388608 | tf_op jit(solution)/shard_map/all_to_all | solution.py:50
  19.1 46.5 %all-to-all-done = bf16[8,1,16,128,128]{4,3,2,1,0:T(8,128)(2,1)} async-done(((bf16[8,1,16,128,128]{4,3,2,1,0:T(8,128)(2,1)}), bf16[8,1,16,128,128]{4,3,2,1,0:T(8,128)(2,1)}, u32[]{:S(2)}, u32[]{:S(2)}) %all-to-all-start) | async-done | bytes 4194336 | tf_op jit(solution)/shard_map/all_to_all | solution.py:50
  65.6 12.9 %gather_fusion.4 = bf16[256,128,128]{2,1,0:T(8,128)(2,1)} fusion(bf16[8,16,128,128]{3,2,1,0:T(8,128)(2,1)} %bitcast.6, s32[256]{0:T(256)S(1)} %reshape.437), kind=kCustom, calls=%fused_computation.4 | custom fusion | bytes 16779264 | tf_op jit(solution)/shard_map/gather | solution.py:52
  78.5 71.2 %all-gather.4.cloned.1.call-done = bf16[32,16,128,128]{3,2,1,0:T(8,128)(2,1)} async-done(((bf16[1,16,128,128]{3,2,1,0:T(8,128)(2,1)}), bf16[32,16,128,128]{3,2,1,0:T(8,128)(2,1)}) %all-gather.4.cloned.1.call-update) | async-done | bytes 16777232 | tf_op jit(solution)/shard_map/all_gather | solution.py:47
  149.7 10.6 %gather_fusion = bf16[16,16,128,128]{3,2,1,0:T(8,128)(2,1)} fusion(bf16[32,16,128,128]{3,2,1,0:T(8,128)(2,1)} %all-gather.4.cloned.1.call-done, s32[1024]{0:T(1024)S(1)} %pad_clamp_fusion.3), kind=kCustom, calls=%fused_computation | custom fusion | bytes 16777280 | tf_op jit(solution)/shard_map/gather | solution.py:48
  160.3 9.0 %fusion.38 = (bf16[16,128,128]{2,1,0:T(8,128)(2,1)}, f32[16,128,128]{2,1,0:T(8,128)S(1)}) fusion(bf16[16,16,128,128]{3,2,1,0:T(8,128)(2,1)} %gather_fusion, bf16[16,16,128,128]{3,2,1,0:T(8,128)(2,1)} %bitcast.92, pred[16,16]{1,0:T(8,128)(4,1)S(1)} %compare_reduce_fusion), kind=kOutput, calls=%fused_computation.88 | convolution fusion | flops 1078198272 | bytes 18350336 | tf_op jit(solution)/shard_map/sltab,sltcb->slac/dot_general | solution.py:54
  169.4 1.9 gather_fusion.5
  171.5 33.0 %all-gather.6.cloned.1.call-done = bf16[128,128,128]{2,1,0:T(8,128)(2,1)} async-done(((bf16[16,128,128]{2,1,0:T(8,128)(2,1)}), bf16[128,128,128]{2,1,0:T(8,128)(2,1)}) %all-gather.6.cloned.1.call-update) | async-done | bytes 4194320 | tf_op jit(solution)/shard_map/all_gather | solution.py:58
  204.5 12.3 %gather_fusion.6 = bf16[256,128,128]{2,1,0:T(8,128)(2,1)} fusion(bf16[8,16,1,128,128]{4,3,1,0,2:T(8,128)(2,1)} %bitcast.91, s32[256]{0:T(256)S(1)} %reshape.453), kind=kCustom, calls=%fused_computation.6 | custom fusion | bytes 16780288 | tf_op jit(solution)/shard_map/gather | solution.py:61
  216.7 8.2 %fusion.17 = f32[16,128,128]{2,1,0:T(8,128)S(1)} fusion(bf16[16,16,128,128]{3,2,1,0:T(8,128)(2,1)} %gather_fusion, bf16[16,16,128,128]{3,2,1,0:T(8,128)(2,1)} %bitcast.93, pred[16,16]{1,0:T(8,128)(4,1)S(1)} %compare_reduce_fusion, f32[16,128,128]{2,1,0:T(8,128)S(1)} %get-tuple-element.23), kind=kOutput, calls=%fused_computation.18 | convolution fusion | flops 1078722560 | bytes 18874624 | tf_op jit(solution)/shard_map/sltab,sltbc->slac/dot_general | solution.py:63
  225.0 0.8 collective-permute-start
  225.8 1.5 collective-permute-start.1
  227.3 1.2 collective-permute-start.2
  228.5 3.2 %collective-permute-start.3 = (f32[1,128,128]{2,1,0:T(8,128)S(1)}, f32[1,128,128]{2,1,0:T(8,128)S(1)}, u32[]{:S(2)}, u32[]{:S(2)}) collective-permute-start(f32[1,128,128]{2,1,0:T(8,128)S(1)} %get-tuple-element.18), channel_id=1, source_target_pairs={{0,2},{1,3},{2,4},{3,5},{4,6},{5,7},{6,8},{7,9},{8,10},{9,11},{10,... | collective-permute-start | bytes 196616 | tf_op jit(solution)/shard_map/ppermute | solution.py:9
  231.8 3.2 %collective-permute-start.4 = (f32[1,128,128]{2,1,0:T(8,128)S(1)}, f32[1,128,128]{2,1,0:T(8,128)S(1)}, u32[]{:S(2)}, u32[]{:S(2)}) collective-permute-start(f32[1,128,128]{2,1,0:T(8,128)S(1)} %get-tuple-element.17), channel_id=1, source_target_pairs={{0,29},{1,30},{2,31},{3,0},{4,1},{5,2},{6,3},{7,4},{8,5},{9,6},{10... | collective-permute-start | bytes 196616 | tf_op jit(solution)/shard_map/ppermute | solution.py:9
  234.9 5.9 %collective-permute-start.6 = (f32[1,128,128]{2,1,0:T(8,128)S(1)}, f32[1,128,128]{2,1,0:T(8,128)S(1)}, u32[]{:S(2)}, u32[]{:S(2)}) collective-permute-start(f32[1,128,128]{2,1,0:T(8,128)S(1)} %get-tuple-element.15), channel_id=1, source_target_pairs={{0,28},{1,29},{2,30},{3,31},{4,0},{5,1},{6,2},{7,3},{8,4},{9,5},{1... | collective-permute-start | bytes 196616 | tf_op jit(solution)/shard_map/ppermute | solution.py:9
  241.0 3.5 %collective-permute-start.8 = (f32[1,128,128]{2,1,0:T(8,128)S(1)}, f32[1,128,128]{2,1,0:T(8,128)S(1)}, u32[]{:S(2)}, u32[]{:S(2)}) collective-permute-start(f32[1,128,128]{2,1,0:T(8,128)S(1)} %get-tuple-element.13), channel_id=1, source_target_pairs={{0,27},{1,28},{2,29},{3,30},{4,31},{5,0},{6,1},{7,2},{8,3},{9,4},{... | collective-permute-start | bytes 196616 | tf_op jit(solution)/shard_map/ppermute | solution.py:9
  244.6 3.8 %collective-permute-start.10 = (f32[1,128,128]{2,1,0:T(8,128)S(1)}, f32[1,128,128]{2,1,0:T(8,128)S(1)}, u32[]{:S(2)}, u32[]{:S(2)}) collective-permute-start(f32[1,128,128]{2,1,0:T(8,128)S(1)} %get-tuple-element.11), channel_id=1, source_target_pairs={{0,26},{1,27},{2,28},{3,29},{4,30},{5,31},{6,0},{7,1},{8,2},{9,3},... | collective-permute-start | bytes 196616 | tf_op jit(solution)/shard_map/ppermute | solution.py:9
  248.3 1.7 collective-permute-start.11
  250.1 10.9 %collective-permute-start.12 = (f32[1,128,128]{2,1,0:T(8,128)S(1)}, f32[1,128,128]{2,1,0:T(8,128)S(1)}, u32[]{:S(2)}, u32[]{:S(2)}) collective-permute-start(f32[1,128,128]{2,1,0:T(8,128)S(1)} %get-tuple-element.9), channel_id=1, source_target_pairs={{0,25},{1,26},{2,27},{3,28},{4,29},{5,30},{6,31},{7,0},{8,1},{9,2}... | collective-permute-start | bytes 196616 | tf_op jit(solution)/shard_map/ppermute | solution.py:9
  261.1 3.0 %collective-permute-start.14 = (f32[1,128,128]{2,1,0:T(8,128)S(1)}, f32[1,128,128]{2,1,0:T(8,128)S(1)}, u32[]{:S(2)}, u32[]{:S(2)}) collective-permute-start(f32[1,128,128]{2,1,0:T(8,128)S(1)} %get-tuple-element.7), channel_id=1, source_target_pairs={{0,16},{1,17},{2,18},{3,19},{4,20},{5,21},{6,22},{7,23},{8,24},{9,... | collective-permute-start | bytes 196616 | tf_op jit(solution)/shard_map/ppermute | solution.py:9
  264.1 5.5 %collective-permute-done.13 = f32[1,128,128]{2,1,0:T(8,128)S(1)} collective-permute-done((f32[1,128,128]{2,1,0:T(8,128)S(1)}, f32[1,128,128]{2,1,0:T(8,128)S(1)}, u32[]{:S(2)}, u32[]{:S(2)}) %collective-permute-start.13) | collective-permute-done | bytes 65568 | tf_op jit(solution)/shard_map/ppermute | solution.py:9
  269.7 1.0 copy-done.2
  (76 shorter events, 5.2 us)
Async XLA Ops:
  6.5 9.6 %copy-start.3 = (s32[16]{0:T(128)S(1)}, s32[16]{0:T(128)}, u32[]{:S(2)}) copy-start(s32[16]{0:T(128)} %constant.118) | copy-start | bytes 196
  6.5 9.5 %copy-start.1 = (s32[256,16]{0,1:T(8,128)S(1)}, s32[256,16]{0,1:T(8,128)}, u32[]{:S(2)}) copy-start(s32[256,16]{0,1:T(8,128)} %param.5) | copy-start | bytes 49156
  6.5 143.2 %all-gather.4.cloned.1.call-start = ((), (), s32[]{:S(2)}) async-start(), calls=%async_computation.1 | async-start | bytes 17301504 | tf_op jit(solution)/shard_map/all_gather | solution.py:47
  11.4 54.2 %all-to-all-start = ((bf16[8,1,16,128,128]{4,3,2,1,0:T(8,128)(2,1)}), bf16[8,1,16,128,128]{4,3,2,1,0:T(8,128)(2,1)}, u32[]{:S(2)}, u32[]{:S(2)}) async-start(bf16[8,1,16,128,128]{4,3,2,1,0:T(8,128)(2,1)} %stack.59), calls=%async_computation | async-start | bytes 8388608 | tf_op jit(solution)/shard_map/all_to_all | solution.py:50
  15.9 188.5 %all-gather.6.cloned.1.call-start = ((), (), s32[]{:S(2)}) async-start(), calls=%async_computation.2 | async-start | bytes 4718592 | tf_op jit(solution)/shard_map/all_gather | solution.py:58
  160.3 9.1 %copy-start = (s32[16]{0:T(128)S(1)}, s32[16]{0:T(128)}, u32[]{:S(2)}) copy-start(s32[16]{0:T(128)} %constant.115.clone) | copy-start | bytes 196
  225.0 9.9 %collective-permute-start = (f32[1,128,128]{2,1,0:T(8,128)S(1)}, f32[1,128,128]{2,1,0:T(8,128)S(1)}, u32[]{:S(2)}, u32[]{:S(2)}) collective-permute-start(f32[1,128,128]{2,1,0:T(8,128)S(1)} %get-tuple-element.21), channel_id=1, source_target_pairs={{0,31},{1,0},{2,1},{3,2},{4,3},{5,4},{6,5},{7,6},{8,7},{9,8},{10,9... | collective-permute-start | bytes 196616 | tf_op jit(solution)/shard_map/ppermute | solution.py:9
  225.8 9.1 %collective-permute-start.1 = (f32[1,128,128]{2,1,0:T(8,128)S(1)}, f32[1,128,128]{2,1,0:T(8,128)S(1)}, u32[]{:S(2)}, u32[]{:S(2)}) collective-permute-start(f32[1,128,128]{2,1,0:T(8,128)S(1)} %get-tuple-element.20), channel_id=1, source_target_pairs={{0,1},{1,2},{2,3},{3,4},{4,5},{5,6},{6,7},{7,8},{8,9},{9,10},{10,1... | collective-permute-start | bytes 196616 | tf_op jit(solution)/shard_map/ppermute | solution.py:9
  227.3 13.5 %collective-permute-start.2 = (f32[1,128,128]{2,1,0:T(8,128)S(1)}, f32[1,128,128]{2,1,0:T(8,128)S(1)}, u32[]{:S(2)}, u32[]{:S(2)}) collective-permute-start(f32[1,128,128]{2,1,0:T(8,128)S(1)} %get-tuple-element.19), channel_id=1, source_target_pairs={{0,30},{1,31},{2,0},{3,1},{4,2},{5,3},{6,4},{7,5},{8,6},{9,7},{10,... | collective-permute-start | bytes 196616 | tf_op jit(solution)/shard_map/ppermute | solution.py:9
  228.5 12.4 %collective-permute-start.3 = (f32[1,128,128]{2,1,0:T(8,128)S(1)}, f32[1,128,128]{2,1,0:T(8,128)S(1)}, u32[]{:S(2)}, u32[]{:S(2)}) collective-permute-start(f32[1,128,128]{2,1,0:T(8,128)S(1)} %get-tuple-element.18), channel_id=1, source_target_pairs={{0,2},{1,3},{2,4},{3,5},{4,6},{5,7},{6,8},{7,9},{8,10},{9,11},{10,... | collective-permute-start | bytes 196616 | tf_op jit(solution)/shard_map/ppermute | solution.py:9
  231.8 12.7 %collective-permute-start.4 = (f32[1,128,128]{2,1,0:T(8,128)S(1)}, f32[1,128,128]{2,1,0:T(8,128)S(1)}, u32[]{:S(2)}, u32[]{:S(2)}) collective-permute-start(f32[1,128,128]{2,1,0:T(8,128)S(1)} %get-tuple-element.17), channel_id=1, source_target_pairs={{0,29},{1,30},{2,31},{3,0},{4,1},{5,2},{6,3},{7,4},{8,5},{9,6},{10... | collective-permute-start | bytes 196616 | tf_op jit(solution)/shard_map/ppermute | solution.py:9
  234.9 9.6 %collective-permute-start.5 = (f32[1,128,128]{2,1,0:T(8,128)S(1)}, f32[1,128,128]{2,1,0:T(8,128)S(1)}, u32[]{:S(2)}, u32[]{:S(2)}) collective-permute-start(f32[1,128,128]{2,1,0:T(8,128)S(1)} %get-tuple-element.16), channel_id=1, source_target_pairs={{0,3},{1,4},{2,5},{3,6},{4,7},{5,8},{6,9},{7,10},{8,11},{9,12},{10... | collective-permute-start | bytes 196616 | tf_op jit(solution)/shard_map/ppermute | solution.py:9
  234.9 13.4 %collective-permute-start.6 = (f32[1,128,128]{2,1,0:T(8,128)S(1)}, f32[1,128,128]{2,1,0:T(8,128)S(1)}, u32[]{:S(2)}, u32[]{:S(2)}) collective-permute-start(f32[1,128,128]{2,1,0:T(8,128)S(1)} %get-tuple-element.15), channel_id=1, source_target_pairs={{0,28},{1,29},{2,30},{3,31},{4,0},{5,1},{6,2},{7,3},{8,4},{9,5},{1... | collective-permute-start | bytes 196616 | tf_op jit(solution)/shard_map/ppermute | solution.py:9
  240.8 9.2 %collective-permute-start.7 = (f32[1,128,128]{2,1,0:T(8,128)S(1)}, f32[1,128,128]{2,1,0:T(8,128)S(1)}, u32[]{:S(2)}, u32[]{:S(2)}) collective-permute-start(f32[1,128,128]{2,1,0:T(8,128)S(1)} %get-tuple-element.14), channel_id=1, source_target_pairs={{0,4},{1,5},{2,6},{3,7},{4,8},{5,9},{6,10},{7,11},{8,12},{9,13},{1... | collective-permute-start | bytes 196616 | tf_op jit(solution)/shard_map/ppermute | solution.py:9
  241.0 20.0 %collective-permute-start.8 = (f32[1,128,128]{2,1,0:T(8,128)S(1)}, f32[1,128,128]{2,1,0:T(8,128)S(1)}, u32[]{:S(2)}, u32[]{:S(2)}) collective-permute-start(f32[1,128,128]{2,1,0:T(8,128)S(1)} %get-tuple-element.13), channel_id=1, source_target_pairs={{0,27},{1,28},{2,29},{3,30},{4,31},{5,0},{6,1},{7,2},{8,3},{9,4},{... | collective-permute-start | bytes 196616 | tf_op jit(solution)/shard_map/ppermute | solution.py:9
  244.4 16.6 %collective-permute-start.9 = (f32[1,128,128]{2,1,0:T(8,128)S(1)}, f32[1,128,128]{2,1,0:T(8,128)S(1)}, u32[]{:S(2)}, u32[]{:S(2)}) collective-permute-start(f32[1,128,128]{2,1,0:T(8,128)S(1)} %get-tuple-element.12), channel_id=1, source_target_pairs={{0,5},{1,6},{2,7},{3,8},{4,9},{5,10},{6,11},{7,12},{8,13},{9,14},{... | collective-permute-start | bytes 196616 | tf_op jit(solution)/shard_map/ppermute | solution.py:9
  244.6 19.5 %collective-permute-start.10 = (f32[1,128,128]{2,1,0:T(8,128)S(1)}, f32[1,128,128]{2,1,0:T(8,128)S(1)}, u32[]{:S(2)}, u32[]{:S(2)}) collective-permute-start(f32[1,128,128]{2,1,0:T(8,128)S(1)} %get-tuple-element.11), channel_id=1, source_target_pairs={{0,26},{1,27},{2,28},{3,29},{4,30},{5,31},{6,0},{7,1},{8,2},{9,3},... | collective-permute-start | bytes 196616 | tf_op jit(solution)/shard_map/ppermute | solution.py:9
  248.3 15.7 %collective-permute-start.11 = (f32[1,128,128]{2,1,0:T(8,128)S(1)}, f32[1,128,128]{2,1,0:T(8,128)S(1)}, u32[]{:S(2)}, u32[]{:S(2)}) collective-permute-start(f32[1,128,128]{2,1,0:T(8,128)S(1)} %get-tuple-element.10), channel_id=1, source_target_pairs={{0,6},{1,7},{2,8},{3,9},{4,10},{5,11},{6,12},{7,13},{8,14},{9,15},... | collective-permute-start | bytes 196616 | tf_op jit(solution)/shard_map/ppermute | solution.py:9
  250.1 14.0 %collective-permute-start.12 = (f32[1,128,128]{2,1,0:T(8,128)S(1)}, f32[1,128,128]{2,1,0:T(8,128)S(1)}, u32[]{:S(2)}, u32[]{:S(2)}) collective-permute-start(f32[1,128,128]{2,1,0:T(8,128)S(1)} %get-tuple-element.9), channel_id=1, source_target_pairs={{0,25},{1,26},{2,27},{3,28},{4,29},{5,30},{6,31},{7,0},{8,1},{9,2}... | collective-permute-start | bytes 196616 | tf_op jit(solution)/shard_map/ppermute | solution.py:9
  261.0 8.7 %collective-permute-start.13 = (f32[1,128,128]{2,1,0:T(8,128)S(1)}, f32[1,128,128]{2,1,0:T(8,128)S(1)}, u32[]{:S(2)}, u32[]{:S(2)}) collective-permute-start(f32[1,128,128]{2,1,0:T(8,128)S(1)} %get-tuple-element.8), channel_id=1, source_target_pairs={{0,7},{1,8},{2,9},{3,10},{4,11},{5,12},{6,13},{7,14},{8,15},{9,16}... | collective-permute-start | bytes 196616 | tf_op jit(solution)/shard_map/ppermute | solution.py:9
  261.1 8.6 %collective-permute-start.14 = (f32[1,128,128]{2,1,0:T(8,128)S(1)}, f32[1,128,128]{2,1,0:T(8,128)S(1)}, u32[]{:S(2)}, u32[]{:S(2)}) collective-permute-start(f32[1,128,128]{2,1,0:T(8,128)S(1)} %get-tuple-element.7), channel_id=1, source_target_pairs={{0,16},{1,17},{2,18},{3,19},{4,20},{5,21},{6,22},{7,23},{8,24},{9,... | collective-permute-start | bytes 196616 | tf_op jit(solution)/shard_map/ppermute | solution.py:9
  269.6 1.0 copy-start.2
Sparse Core Ops, SparseCore 0:
  9.9 139.7 all-gather.3
  169.4 35.0 all-gather.5
